TPU v7x, 32 devices: a whole 2x2x4 slice. The times are simulated.
32 devices in a mesh: hyd: 4 (over y, x), src: 8 (over z, core).
Axes of the slice: x: 2, y: 2, z: 4, core: 2. Of those that a mesh axis runs over, the one named last changes fastest.
Arguments:
- record: float32 [2, 4096, 128], P(None, 'hyd'), may hold values from -6 to 6
- tile_data: bfloat16 [4, 8, 24, 2, 128, 128], P('hyd', 'src'), may hold values from -0.125 to 0.125
- tile_rows: int32 [4, 8, 24], P('hyd', 'src'), may hold values from 0 to 7, as said below
- tile_cols: int32 [4, 8, 24], P('hyd', 'src'), may hold values from 0 to 7, as said below
- tile_counts: int32 [4, 8], P('hyd', 'src'), may hold values from 3 to 24, as said below
Outputs:
- solution: float32 [2, 8192, 128], P(None, 'src')
- residual: float32 [2, 4096, 128], P(None, 'hyd')
Inputs may be any that keep to these rules, and one draw needn't show every extreme that they name: `tile_rows`: together with tile_cols, the 24 slots of one device name different tile pairs. `tile_cols`: column tiles below 4 belong to the upper layer. `tile_counts`: slots at and beyond a device's count hold no tiles of A.
All inputs are finite; a program needn't handle non-finite values.
Results may differ from a plain program's by a relative error of at most 0.014.
Values may be sent and summed in bfloat16 or wider, within the bound.
No kernel may reach another device: no remote copies, remote signals or barrier semaphores. Data moves between devices by JAX's collectives and lax.ppermute only.
A program may use at most 64 MiB of HBM per device.

v0:
```python
import jax
import jax.numpy as jnp
from jax import lax
from jax.sharding import PartitionSpec as P

SRC_DEV = 512
ITERS = 3
EPSILON = 1e-06


def place_tiles(total, products, target, usable):
    for slot in range(products.shape[1]):
        current = lax.dynamic_slice_in_dim(total, target[slot], 1, 1)
        added = current + products[:, slot][:, None] * usable[slot]
        total = lax.dynamic_update_slice_in_dim(total, added, target[slot], 1)
    return total


def tile_forward(tile_group_all, rows_list, cols_list, first_slot, end_slot, vector_b, row_tiles):
    group_slots = 8
    tile_size = tile_group_all.shape[-1]
    shot_count = vector_b.shape[2]
    col_tiles = vector_b.shape[1] // tile_size
    blocks = vector_b.reshape(2, col_tiles, tile_size, shot_count)

    def one_turn(group, total):
        start = group * group_slots
        tile_group = lax.dynamic_slice_in_dim(tile_group_all, start, group_slots, 0)
        col_pick = lax.dynamic_slice_in_dim(cols_list, start, group_slots, 0)
        row_pick = lax.dynamic_slice_in_dim(rows_list, start, group_slots, 0)
        slot_ids = start + jnp.arange(group_slots)
        usable = ((slot_ids >= first_slot) & (slot_ids < end_slot)).astype(jnp.float32)
        chosen = jnp.take(blocks, col_pick, axis=1)
        real_part = jnp.einsum(
            "gij,gjn->gin", tile_group[:, 0], chosen[0], preferred_element_type=jnp.float32
        ) - jnp.einsum(
            "gij,gjn->gin", tile_group[:, 1], chosen[1], preferred_element_type=jnp.float32
        )
        imag_part = jnp.einsum(
            "gij,gjn->gin", tile_group[:, 0], chosen[1], preferred_element_type=jnp.float32
        ) + jnp.einsum(
            "gij,gjn->gin", tile_group[:, 1], chosen[0], preferred_element_type=jnp.float32
        )
        return place_tiles(total, jnp.stack([real_part, imag_part]), row_pick, usable)

    empty = jnp.zeros((2, row_tiles, tile_size, shot_count), jnp.float32)
    result = lax.fori_loop(
        first_slot // group_slots, (end_slot + group_slots - 1) // group_slots, one_turn, empty
    )
    return result.reshape(2, row_tiles * tile_size, shot_count)


def tile_adjoint(tile_group_all, rows_list, cols_list, first_slot, end_slot, residual_b, col_tiles):
    group_slots = 8
    tile_size = tile_group_all.shape[-1]
    shot_count = residual_b.shape[2]
    row_tiles = residual_b.shape[1] // tile_size
    blocks = residual_b.reshape(2, row_tiles, tile_size, shot_count)

    def one_turn(group, total):
        start = group * group_slots
        tile_group = lax.dynamic_slice_in_dim(tile_group_all, start, group_slots, 0)
        col_pick = lax.dynamic_slice_in_dim(cols_list, start, group_slots, 0)
        row_pick = lax.dynamic_slice_in_dim(rows_list, start, group_slots, 0)
        slot_ids = start + jnp.arange(group_slots)
        usable = ((slot_ids >= first_slot) & (slot_ids < end_slot)).astype(jnp.float32)
        chosen = jnp.take(blocks, row_pick, axis=1)
        real_part = jnp.einsum(
            "gji,gjn->gin", tile_group[:, 0], chosen[0], preferred_element_type=jnp.float32
        ) + jnp.einsum(
            "gji,gjn->gin", tile_group[:, 1], chosen[1], preferred_element_type=jnp.float32
        )
        imag_part = jnp.einsum(
            "gji,gjn->gin", tile_group[:, 0], chosen[1], preferred_element_type=jnp.float32
        ) - jnp.einsum(
            "gji,gjn->gin", tile_group[:, 1], chosen[0], preferred_element_type=jnp.float32
        )
        return place_tiles(total, jnp.stack([real_part, imag_part]), col_pick, usable)

    empty = jnp.zeros((2, col_tiles, tile_size, shot_count), jnp.float32)
    result = lax.fori_loop(
        first_slot // group_slots, (end_slot + group_slots - 1) // group_slots, one_turn, empty
    )
    return result.reshape(2, col_tiles * tile_size, shot_count)


def body(record, tile_data, tile_rows, tile_cols, tile_counts):
    own_tiles = tile_data[0, 0]
    own_rows = tile_rows[0, 0]
    own_cols = tile_cols[0, 0]
    own_count = tile_counts[0, 0]
    tile_size = own_tiles.shape[-1]
    row_tiles = record.shape[1] // tile_size
    col_tiles = 2 * SRC_DEV // tile_size

    def gradient_of(residual_b):
        partial_value = tile_adjoint(
            own_tiles, own_rows, own_cols, 0, own_count, residual_b, col_tiles
        )
        gradient = lax.psum(partial_value, "hyd")
        squares = lax.psum(jnp.sum(gradient * gradient, axis=(0, 1)), "src")
        return (gradient, squares)

    residual = record
    gradient, gamma_now = gradient_of(record.astype(jnp.bfloat16))
    direction = gradient
    solution = jnp.zeros_like(gradient)
    for step_index in range(ITERS):
        direction_b = direction.astype(jnp.bfloat16)
        forward_partial_value = tile_forward(
            own_tiles, own_rows, own_cols, 0, own_count, direction_b, row_tiles
        )
        image = lax.psum(forward_partial_value, "src")
        image_sq = lax.psum(jnp.sum(image * image, axis=(0, 1)), "hyd")
        image, image_sq = (image, image_sq)
        alpha_step = gamma_now / (image_sq + EPSILON)
        solution = solution + alpha_step * direction
        residual = residual - alpha_step * image
        if step_index + 1 < ITERS:
            residual_b = residual.astype(jnp.bfloat16)
            gradient, gamma_next = gradient_of(residual_b)
            direction = gradient + gamma_next / (gamma_now + EPSILON) * direction
            gamma_now = gamma_next
    return (solution, residual)


def solution(mesh):
    in_specs = (
        P(None, "hyd", None),
        P("hyd", "src", None, None, None, None),
        P("hyd", "src", None),
        P("hyd", "src", None),
        P("hyd", "src"),
    )
    out_specs = (P(None, "src", None), P(None, "hyd", None))
    return jax.shard_map(body, mesh=mesh, in_specs=in_specs, out_specs=out_specs, check_vma=False)
```

profile of v0, /device:TPU:0, one launch (start us, length us, event | category | flops | bytes accessed | tf_op | source)
XLA Modules:
  0.0 1104.4 jit_solution(888676539581461893)
XLA Ops:
  7.9 2.7 copy.18
  11.3 28.1 %while.60 = (s32[]{:T(128)}, f32[2,8,128,128]{3,2,1,0:T(8,128)S(1)}, s32[]{:T(128)}, s32[24]{0:T(128)S(1)}, bf16[24,2,128,128]{2,3,0,1:T(8,128)(2,1)}, /*index=5...) while((s32[]{:T(128)}, ...), condition=%wide.region_1.3_spmd, body=%wide.region_0.2_spmd.sunk | while | flops 135529568 | bytes 17830816 | solution.py:81
  41.9 108.4 %all-reduce.7.cloned.1.call-done = f32[2,1024,128]{2,1,0:T(8,128)} async-done(((f32[2,1024,128]{2,1,0:T(8,128)}), f32[2,1024,128]{2,1,0:T(8,128)}) %all-reduce.7.cloned.1.call-update) | async-done | bytes 1048592 | tf_op jit(solution)/shard_map/psum | solution.py:100
  150.3 2.5 multiply_reduce_fusion.5
  153.9 38.0 %while.61 = (s32[]{:T(128)}, f32[2,8,128,128]{3,2,1,0:T(8,128)}, s32[]{:T(128)}, s32[24]{0:T(128)S(1)}, bf16[24,2,128,128]{3,2,0,1:T(8,128)(2,1)S(1)}, /*index=5...) while((s32[]{:T(128)}, f32[2,8,128,128]{3,2,1,0:T(8,128)}, ...), condition=%wide.region_6.8_spmd, body=%wide.region_5.7_spmd.sunk | while | flops 135529568 | bytes 17834880 | solution.py:47
  160.6 2.3 fusion.368
  164.8 2.2 fusion.369
  169.1 2.1 fusion.370
  173.1 2.1 fusion.371
  177.4 2.2 fusion.372
  181.6 2.2 fusion.373
  185.8 2.3 fusion.374
  189.8 2.2 fusion.375
  192.0 92.6 %psum.85 = f32[128]{0:T(128)S(1)} all-reduce(f32[128]{0:T(128)S(1)} %get-tuple-element.527), channel_id=1, replica_groups=mesh['hyd'=4,'src'=8] {'src'}, use_global_device_ids=true, to_apply=%region_4.6 | all-reduce | flops 128 | bytes 1024 | tf_op jit(solution)/shard_map/psum | solution.py:101
  284.6 42.1 %all-reduce.9.cloned.1.call-done = f32[2,1024,128]{2,1,0:T(8,128)} async-done(((f32[2,1024,128]{2,1,0:T(8,128)}), f32[2,1024,128]{2,1,0:T(8,128)}) %all-reduce.9.cloned.1.call-update) | async-done | bytes 1048592 | tf_op jit(solution)/shard_map/psum | solution.py:113
  328.2 9.8 psum.87
  338.0 2.1 fusion.241
  341.2 41.8 %while.62 = (s32[]{:T(128)}, f32[2,8,128,128]{3,2,1,0:T(8,128)}, s32[]{:T(128)}, s32[24]{0:T(128)S(1)}, bf16[24,2,128,128]{2,3,0,1:T(8,128)(2,1)}, /*index=5*/s3...) while((s32[]{:T(128)}, f32[2,8,128,128]{3,2,1,0:T(8,128)}, ...), condition=%wide.region_11.13_spmd, body=%wide.region_10.12_spmd.sunk | while | flops 135529568 | bytes 17834880 | solution.py:81
  351.6 2.3 fusion.383
  355.9 2.2 fusion.384
  360.2 2.1 fusion.385
  364.2 2.1 fusion.386
  368.4 2.2 fusion.387
  372.7 2.2 fusion.388
  376.9 2.3 fusion.389
  380.8 2.2 fusion.390
  383.1 132.6 %all-reduce.11.cloned.1.call-done = f32[2,1024,128]{2,1,0:T(8,128)} async-done(((f32[2,1024,128]{2,1,0:T(8,128)}), f32[2,1024,128]{2,1,0:T(8,128)}) %all-reduce.11.cloned.1.call-update) | async-done | bytes 1048592 | tf_op jit(solution)/shard_map/psum | solution.py:100
  517.2 16.2 %psum.89 = f32[128]{0:T(128)S(1)} all-reduce(f32[128]{0:T(128)S(1)} %multiply_reduce_fusion.3), channel_id=1, replica_groups=mesh['hyd'=4,'src'=8] {'src'}, use_global_device_ids=true, to_apply=%region_14.16 | all-reduce | flops 128 | bytes 1024 | tf_op jit(solution)/shard_map/psum | solution.py:101
  533.4 2.1 fusion.242
  536.6 38.0 %while.63 = (s32[]{:T(128)}, f32[2,8,128,128]{3,2,1,0:T(8,128)}, s32[]{:T(128)}, s32[24]{0:T(128)S(1)}, bf16[24,2,128,128]{3,2,0,1:T(8,128)(2,1)S(1)}, /*index=5...) while((s32[]{:T(128)}, f32[2,8,128,128]{3,2,1,0:T(8,128)}, ...), condition=%wide.region_16.18_spmd, body=%wide.region_15.17_spmd.sunk | while | flops 135529568 | bytes 17834880 | solution.py:47
  543.6 2.2 fusion.398
  547.8 2.2 fusion.399
  552.0 2.2 fusion.400
  556.1 2.3 fusion.401
  564.2 2.2 fusion.403
  568.2 2.1 fusion.404
  572.3 2.3 fusion.405
  574.7 131.5 %all-reduce.13.cloned.1.call-done = f32[2,1024,128]{2,1,0:T(8,128)} async-done(((f32[2,1024,128]{2,1,0:T(8,128)}), f32[2,1024,128]{2,1,0:T(8,128)}) %all-reduce.13.cloned.1.call-update) | async-done | bytes 1048592 | tf_op jit(solution)/shard_map/psum | solution.py:113
  707.7 9.8 psum.91
  717.5 2.9 fusion.243
  721.4 41.1 %while.64 = (s32[]{:T(128)}, f32[2,8,128,128]{3,2,1,0:T(8,128)}, s32[]{:T(128)}, s32[24]{0:T(128)S(1)}, bf16[24,2,128,128]{2,3,0,1:T(8,128)(2,1)}, /*index=5*/s3...) while((s32[]{:T(128)}, f32[2,8,128,128]{3,2,1,0:T(8,128)}, ...), condition=%wide.region_21.23_spmd, body=%wide.region_20.22_spmd.sunk | while | flops 135529568 | bytes 17834880 | solution.py:81
  732.0 2.2 fusion.413
  736.0 2.3 fusion.414
  740.0 2.2 fusion.415
  743.9 2.1 fusion.416
  748.1 2.2 fusion.417
  752.1 2.2 fusion.418
  756.1 2.3 fusion.419
  760.3 2.2 fusion.420
  762.6 131.3 %all-reduce.15.cloned.1.call-done = f32[2,1024,128]{2,1,0:T(8,128)} async-done(((f32[2,1024,128]{2,1,0:T(8,128)}), f32[2,1024,128]{2,1,0:T(8,128)}) %all-reduce.15.cloned.1.call-update) | async-done | bytes 1048592 | tf_op jit(solution)/shard_map/psum | solution.py:100
  895.4 16.2 %psum.93 = f32[128]{0:T(128)S(1)} all-reduce(f32[128]{0:T(128)S(1)} %multiply_reduce_fusion.1), channel_id=1, replica_groups=mesh['hyd'=4,'src'=8] {'src'}, use_global_device_ids=true, to_apply=%region_24.26 | all-reduce | flops 128 | bytes 1024 | tf_op jit(solution)/shard_map/psum | solution.py:101
  911.6 2.5 fusion.240
  915.2 37.3 %while.65 = (s32[]{:T(128)}, f32[2,8,128,128]{3,2,1,0:T(8,128)}, s32[]{:T(128)}, s32[24]{0:T(128)S(1)}, bf16[24,2,128,128]{3,2,0,1:T(8,128)(2,1)S(1)}, /*index=5...) while((s32[]{:T(128)}, f32[2,8,128,128]{3,2,1,0:T(8,128)}, ...), condition=%wide.region_26.28_spmd, body=%wide.region_25.27_spmd.sunk | while | flops 135529568 | bytes 17834880 | solution.py:47
  921.9 2.2 fusion.428
  926.0 2.3 fusion.429
  930.0 2.2 fusion.430
  933.8 2.1 fusion.431
  938.0 2.2 fusion.432
  942.1 2.2 fusion.433
  946.1 2.3 fusion.434
  950.3 2.2 fusion.435
  952.5 130.2 %all-reduce.17.cloned.1.call-done = f32[2,1024,128]{2,1,0:T(8,128)} async-done(((f32[2,1024,128]{2,1,0:T(8,128)}), f32[2,1024,128]{2,1,0:T(8,128)}) %all-reduce.17.cloned.1.call-update) | async-done | bytes 1048592 | tf_op jit(solution)/shard_map/psum | solution.py:113
  1084.2 9.8 psum.95
  1094.0 3.6 multiply_subtract_fusion
  (125 shorter events, 63.3 us)
Async XLA Ops:
  7.2 143.2 %all-reduce.7.cloned.1.call-start = ((), (), s32[]{:S(2)}) async-start(), calls=%async_computation | async-start | bytes 2097152 | tf_op jit(solution)/shard_map/psum | solution.py:100
  7.9 2.7 copy-start.5
  10.6 0.7 copy-start.8
  10.6 0.7 copy-start.9
  39.3 1.0 copy-start
  40.3 286.4 %all-reduce.9.cloned.1.call-start = ((), (), s32[]{:S(2)}) async-start(), calls=%async_computation.1 | async-start | bytes 2097152 | tf_op jit(solution)/shard_map/psum | solution.py:113
  191.9 146.1 %copy-start.6 = (f32[2,1024,128]{2,1,0:T(8,128)S(1)}, f32[2,1024,128]{2,1,0:T(8,128)}, u32[]{:S(2)}) copy-start(f32[2,1024,128]{2,1,0:T(8,128)} %param.19) | copy-start | bytes 3145732
  192.0 323.8 %all-reduce.11.cloned.1.call-start = ((), (), s32[]{:S(2)}) async-start(), calls=%async_computation.2 | async-start | bytes 2097152 | tf_op jit(solution)/shard_map/psum | solution.py:100
  383.0 150.4 %copy-start.1 = (f32[2,1024,128]{2,1,0:T(8,128)S(1)}, f32[2,1024,128]{2,1,0:T(8,128)}, u32[]{:S(2)}) copy-start(f32[2,1024,128]{2,1,0:T(8,128)} %all-reduce.7.cloned.1.call-done) | copy-start | bytes 3145732
  383.0 323.1 %all-reduce.13.cloned.1.call-start = ((), (), s32[]{:S(2)}) async-start(), calls=%async_computation.3 | async-start | bytes 2097152 | tf_op jit(solution)/shard_map/psum | solution.py:113
  574.6 142.8 %copy-start.7 = (f32[2,1024,128]{2,1,0:T(8,128)S(1)}, f32[2,1024,128]{2,1,0:T(8,128)}, u32[]{:S(2)}) copy-start(f32[2,1024,128]{2,1,0:T(8,128)} %param.19) | copy-start | bytes 3145732
  574.6 319.2 %all-reduce.15.cloned.1.call-start = ((), (), s32[]{:S(2)}) async-start(), calls=%async_computation.4 | async-start | bytes 2097152 | tf_op jit(solution)/shard_map/psum | solution.py:100
  762.5 149.0 %copy-start.2 = (f32[2,1024,128]{2,1,0:T(8,128)S(1)}, f32[2,1024,128]{2,1,0:T(8,128)}, u32[]{:S(2)}) copy-start(f32[2,1024,128]{2,1,0:T(8,128)} %all-reduce.7.cloned.1.call-done) | copy-start | bytes 3145732
  762.6 320.1 %all-reduce.17.cloned.1.call-start = ((), (), s32[]{:S(2)}) async-start(), calls=%async_computation.5 | async-start | bytes 2097152 | tf_op jit(solution)/shard_map/psum | solution.py:113
  952.5 141.5 %copy-start.3 = (f32[2,1024,128]{2,1,0:T(8,128)S(1)}, f32[2,1024,128]{2,1,0:T(8,128)}, u32[]{:S(2)}) copy-start(f32[2,1024,128]{2,1,0:T(8,128)} %all-reduce.7.cloned.1.call-done) | copy-start | bytes 3145732
  952.5 141.5 %copy-start.4 = (f32[2,1024,128]{2,1,0:T(8,128)S(1)}, f32[2,1024,128]{2,1,0:T(8,128)}, u32[]{:S(2)}) copy-start(f32[2,1024,128]{2,1,0:T(8,128)} %all-reduce.11.cloned.1.call-done) | copy-start | bytes 3145732
Sparse Core Ops, SparseCore 0:
  40.4 109.8 all-reduce.6
  192.1 134.5 all-reduce.8
  383.1 132.5 all-reduce.10
  574.8 131.3 all-reduce.12
  762.7 131.1 all-reduce.14
  952.6 130.0 all-reduce.16
where the time goes:
time: 1110 us; the launch traced here: 1100 us
  waiting for transfers between devices  676 us (61%)
  blocking collectives  154 us (14%)
  other arithmetic  122 us (11%)
  loops' own time  91.6 us (8%)
  local copies, waits for them, and re-layouts  29 us (3%)
  matrix products  16.7 us (2%)
  between operations  14.9 us (1%)
    psum x3, waiting for transfers between devices, gradient_of(): gradient = lax.psum(partial_value, 'hyd')  372 us
    psum x3, waiting for transfers between devices, body(): image = lax.psum(forward_partial_value, 'src')  304 us
    psum x3, blocking collectives, gradient_of(): squares = lax.psum(jnp.sum(gradient * gradient, axis=(0, 1)), 'src')  125 us
    dynamic_update_slice x48, other arithmetic, place_tiles(): total = lax.dynamic_update_slice_in_dim(total, added, target[slot], 1)  93.1 us
    another operation x3, loops' own time, tile_forward(): lax.fori_loop(first_slot // group_slots, (end_slot + group_slots - 1) //...  45.9 us
    another operation x3, loops' own time, tile_adjoint(): lax.fori_loop(first_slot // group_slots, (end_slot + group_slots - 1) //...  45.7 us
    psum x3, blocking collectives, body(): image_sq = lax.psum(jnp.sum(image * image, axis=(0, 1)), 'hyd')  29.3 us
  transfers between devices with their start and end apart: 6, of which 6 were waited for; matrix products, arithmetic and copies ran while one was open for 0% of the time, Pallas kernels for 0%

commit v1 on v0

--- a/solution.py
+++ b/solution.py
@@ -110,7 +110,9 @@
         forward_partial_value = tile_forward(
             own_tiles, own_rows, own_cols, 0, own_count, direction_b, row_tiles
         )
-        image = lax.psum(forward_partial_value, "src")
+        image = forward_partial_value
+        for hop in (1, 2, 4):
+            image = image + lax.ppermute(image, "src", [(dev, dev ^ hop) for dev in range(8)])
         image_sq = lax.psum(jnp.sum(image * image, axis=(0, 1)), "hyd")
         image, image_sq = (image, image_sq)
         alpha_step = gamma_now / (image_sq + EPSILON)

time: 1110 us -> 1170 us (1.054)
  starting transfers between devices: 0.24 us -> 230 us
  waiting for transfers between devices: 676 us -> 560 us
  blocking collectives: 154 us -> 93.4 us
    psum x3 -> x0, waiting for transfers between devices: 304 us -> none  [body(): image = lax.psum(forward_partial_value, 'src')]
    ppermute x0 -> x9, starting transfers between devices: none -> 230 us  [body(): lax.ppermute(image, 'src', [(dev, dev ^ hop) for dev in range(8)])]
    ppermute x0 -> x9, waiting for transfers between devices: none -> 182 us  [body(): lax.ppermute(image, 'src', [(dev, dev ^ hop) for dev in range(8)])]
    psum x3, blocking collectives: 125 us -> 66.7 us  [gradient_of(): squares = lax.psum(jnp.sum(gradient * gradient, axis=(0, 1)), 'src')]
  transfers between devices with their start and end apart: 6 -> 12, of which waited for: 6 -> 12; matrix products, arithmetic and copies ran while one was open for 0% -> 0% of each run, Pallas kernels for 0% -> 0%
where the time goes in v1:
time: 1170 us; the launch traced here: 1160 us
  waiting for transfers between devices  560 us (48%)
  starting transfers between devices  230 us (20%)
  other arithmetic  130 us (11%)
  blocking collectives  93.4 us (8%)
  loops' own time  90.7 us (8%)
  local copies, waits for them, and re-layouts  29 us (2%)
  matrix products  16.7 us (1%)
  between operations  14.5 us (1%)
    psum x3, waiting for transfers between devices, gradient_of(): gradient = lax.psum(partial_value, 'hyd')  378 us
    ppermute x9, starting transfers between devices, body(): lax.ppermute(image, 'src', [(dev, dev ^ hop) for dev in range(8)])  230 us
    ppermute x9, waiting for transfers between devices, body(): lax.ppermute(image, 'src', [(dev, dev ^ hop) for dev in range(8)])  182 us
    dynamic_update_slice x48, other arithmetic, place_tiles(): total = lax.dynamic_update_slice_in_dim(total, added, target[slot], 1)  93.4 us
    psum x3, blocking collectives, gradient_of(): squares = lax.psum(jnp.sum(gradient * gradient, axis=(0, 1)), 'src')  66.7 us
    another operation x3, loops' own time, tile_adjoint(): lax.fori_loop(first_slot // group_slots, (end_slot + group_slots - 1) //...  46 us
    another operation x3, loops' own time, tile_forward(): lax.fori_loop(first_slot // group_slots, (end_slot + group_slots - 1) //...  44.7 us
    psum x3, blocking collectives, body(): image_sq = lax.psum(jnp.sum(image * image, axis=(0, 1)), 'hyd')  26.7 us
  transfers between devices with their start and end apart: 12, of which 12 were waited for; matrix products, arithmetic and copies ran while one was open for 0% of the time, Pallas kernels for 0%

profile of v1, /device:TPU:0, one launch (start us, length us, event | category | flops | bytes accessed | tf_op | source)
XLA Modules:
  0.0 1164.4 jit_solution(5365696861917652262)
XLA Ops:
  7.9 2.7 copy.18
  11.3 28.3 %while.60 = (s32[]{:T(128)}, f32[2,8,128,128]{3,2,1,0:T(8,128)S(1)}, s32[]{:T(128)}, s32[24]{0:T(128)S(1)}, bf16[24,2,128,128]{2,3,0,1:T(8,128)(2,1)}, /*index=5...) while((s32[]{:T(128)}, ...), condition=%wide.region_1.3_spmd, body=%wide.region_0.2_spmd.sunk | while | flops 135529568 | bytes 17830816 | solution.py:81
  42.3 109.0 %all-reduce.4.cloned.1.call-done = f32[2,1024,128]{2,1,0:T(8,128)} async-done(((f32[2,1024,128]{2,1,0:T(8,128)}), f32[2,1024,128]{2,1,0:T(8,128)}) %all-reduce.4.cloned.1.call-update) | async-done | bytes 1048592 | tf_op jit(solution)/shard_map/psum | solution.py:100
  151.2 2.5 multiply_reduce_fusion.5
  154.8 37.0 %while.61 = (s32[]{:T(128)}, f32[2,8,128,128]{3,2,1,0:T(8,128)}, s32[]{:T(128)}, s32[24]{0:T(128)S(1)}, bf16[24,2,128,128]{3,2,0,1:T(8,128)(2,1)S(1)}, /*index=5...) while((s32[]{:T(128)}, f32[2,8,128,128]{3,2,1,0:T(8,128)}, ...), condition=%wide.region_6.8_spmd, body=%wide.region_5.7_spmd.sunk | while | flops 135529568 | bytes 17834880 | solution.py:47
  165.5 2.3 fusion.369
  173.7 2.2 fusion.371
  189.6 2.2 fusion.375
  191.8 36.6 %collective-permute-start = (f32[2,1024,128]{2,1,0:T(8,128)}, f32[2,1024,128]{2,1,0:T(8,128)S(1)}, u32[]{:S(2)}, u32[]{:S(2)}) collective-permute-start(f32[2,1024,128]{2,1,0:T(8,128)} %bitcast.579), channel_id=1, source_target_pairs={{0,1},{1,0},{2,3},{3,2},{4,5},{5,4},{6,7},{7,6},{8,9},{9,8},{10,11... | collective-permute-start | bytes 3145736 | tf_op jit(solution)/shard_map/ppermute | solution.py:115
  228.4 2.5 collective-permute-done
  232.3 39.2 %collective-permute-start.1 = (f32[2,1024,128]{2,1,0:T(8,128)S(1)}, f32[2,1024,128]{2,1,0:T(8,128)S(1)}, u32[]{:S(2)}, u32[]{:S(2)}) collective-permute-start(f32[2,1024,128]{2,1,0:T(8,128)S(1)} %bitcast_add_fusion.2), channel_id=1, source_target_pairs={{0,2},{1,3},{2,0},{3,1},{4,6},{5,7},{6,4},{7,5},{8,10},{9,11},{10,... | collective-permute-start | bytes 3145736 | tf_op jit(solution)/shard_map/ppermute | solution.py:115
  271.5 23.5 %collective-permute-done.1 = f32[2,1024,128]{2,1,0:T(8,128)S(1)} collective-permute-done((f32[2,1024,128]{2,1,0:T(8,128)S(1)}, f32[2,1024,128]{2,1,0:T(8,128)S(1)}, u32[]{:S(2)}, u32[]{:S(2)}) %collective-permute-start.1) | collective-permute-done | bytes 1048608 | tf_op jit(solution)/shard_map/ppermute | solution.py:115
  298.0 34.4 %psum.64 = f32[128]{0:T(128)S(1)} all-reduce(f32[128]{0:T(128)S(1)} %get-tuple-element.533), channel_id=1, replica_groups=mesh['hyd'=4,'src'=8] {'src'}, use_global_device_ids=true, to_apply=%region_4.6 | all-reduce | flops 128 | bytes 1024 | tf_op jit(solution)/shard_map/psum | solution.py:101
  332.3 12.2 %collective-permute-done.2 = f32[2,1024,128]{2,1,0:T(8,128)} collective-permute-done((f32[2,1024,128]{2,1,0:T(8,128)}, f32[2,1024,128]{2,1,0:T(8,128)}, u32[]{:S(2)}, u32[]{:S(2)}) %collective-permute-start.2) | collective-permute-done | bytes 1048608 | tf_op jit(solution)/shard_map/ppermute | solution.py:115
  344.6 2.7 multiply_reduce_fusion.4
  347.3 8.9 psum.65
  359.4 41.5 %while.62 = (s32[]{:T(128)}, f32[2,8,128,128]{3,2,1,0:T(8,128)}, s32[]{:T(128)}, s32[24]{0:T(128)S(1)}, bf16[24,2,128,128]{2,3,0,1:T(8,128)(2,1)}, /*index=5*/s3...) while((s32[]{:T(128)}, f32[2,8,128,128]{3,2,1,0:T(8,128)}, ...), condition=%wide.region_10.12_spmd, body=%wide.region_9.11_spmd.sunk | while | flops 135529568 | bytes 17834880 | solution.py:81
  370.2 2.2 fusion.383
  374.1 2.2 fusion.384
  394.5 2.2 fusion.389
  398.6 2.3 fusion.390
  401.0 136.8 %all-reduce.6.cloned.1.call-done = f32[2,1024,128]{2,1,0:T(8,128)} async-done(((f32[2,1024,128]{2,1,0:T(8,128)}), f32[2,1024,128]{2,1,0:T(8,128)}) %all-reduce.6.cloned.1.call-update) | async-done | bytes 1048592 | tf_op jit(solution)/shard_map/psum | solution.py:100
  539.2 16.2 %psum.67 = f32[128]{0:T(128)S(1)} all-reduce(f32[128]{0:T(128)S(1)} %multiply_reduce_fusion.3), channel_id=1, replica_groups=mesh['hyd'=4,'src'=8] {'src'}, use_global_device_ids=true, to_apply=%region_13.15 | all-reduce | flops 128 | bytes 1024 | tf_op jit(solution)/shard_map/psum | solution.py:101
  558.6 37.7 %while.63 = (s32[]{:T(128)}, f32[2,8,128,128]{3,2,1,0:T(8,128)}, s32[]{:T(128)}, s32[24]{0:T(128)S(1)}, bf16[24,2,128,128]{3,2,0,1:T(8,128)(2,1)S(1)}, /*index=5...) while((s32[]{:T(128)}, f32[2,8,128,128]{3,2,1,0:T(8,128)}, ...), condition=%wide.region_15.17_spmd, body=%wide.region_14.16_spmd.sunk | while | flops 135529568 | bytes 17834880 | solution.py:47
  565.4 2.2 fusion.398
  569.6 2.2 fusion.399
  573.7 2.2 fusion.400
  577.8 2.3 fusion.401
  585.9 2.3 fusion.403
  589.9 2.3 fusion.404
  594.2 2.2 fusion.405
  596.4 35.0 %collective-permute-start.3 = (f32[2,1024,128]{2,1,0:T(8,128)}, f32[2,1024,128]{2,1,0:T(8,128)S(1)}, u32[]{:S(2)}, u32[]{:S(2)}) collective-permute-start(f32[2,1024,128]{2,1,0:T(8,128)} %bitcast.580), channel_id=1, source_target_pairs={{0,1},{1,0},{2,3},{3,2},{4,5},{5,4},{6,7},{7,6},{8,9},{9,8},{10,11... | collective-permute-start | bytes 3145736 | tf_op jit(solution)/shard_map/ppermute | solution.py:115
  631.4 2.5 collective-permute-done.3
  635.2 38.9 %collective-permute-start.4 = (f32[2,1024,128]{2,1,0:T(8,128)S(1)}, f32[2,1024,128]{2,1,0:T(8,128)S(1)}, u32[]{:S(2)}, u32[]{:S(2)}) collective-permute-start(f32[2,1024,128]{2,1,0:T(8,128)S(1)} %bitcast_add_fusion.1), channel_id=1, source_target_pairs={{0,2},{1,3},{2,0},{3,1},{4,6},{5,7},{6,4},{7,5},{8,10},{9,11},{10,... | collective-permute-start | bytes 3145736 | tf_op jit(solution)/shard_map/ppermute | solution.py:115
  674.1 23.5 %collective-permute-done.4 = f32[2,1024,128]{2,1,0:T(8,128)S(1)} collective-permute-done((f32[2,1024,128]{2,1,0:T(8,128)S(1)}, f32[2,1024,128]{2,1,0:T(8,128)S(1)}, u32[]{:S(2)}, u32[]{:S(2)}) %collective-permute-start.4) | collective-permute-done | bytes 1048608 | tf_op jit(solution)/shard_map/ppermute | solution.py:115
  698.6 2.3 collective-permute-start.5
  700.9 46.0 %collective-permute-done.5 = f32[2,1024,128]{2,1,0:T(8,128)} collective-permute-done((f32[2,1024,128]{2,1,0:T(8,128)}, f32[2,1024,128]{2,1,0:T(8,128)}, u32[]{:S(2)}, u32[]{:S(2)}) %collective-permute-start.5) | collective-permute-done | bytes 1048608 | tf_op jit(solution)/shard_map/ppermute | solution.py:115
  746.9 2.7 multiply_reduce_fusion.2
  749.7 8.9 psum.68
  758.6 2.9 fusion.243
  762.5 41.5 %while.64 = (s32[]{:T(128)}, f32[2,8,128,128]{3,2,1,0:T(8,128)}, s32[]{:T(128)}, s32[24]{0:T(128)S(1)}, bf16[24,2,128,128]{2,3,0,1:T(8,128)(2,1)}, /*index=5*/s3...) while((s32[]{:T(128)}, f32[2,8,128,128]{3,2,1,0:T(8,128)}, ...), condition=%wide.region_19.21_spmd, body=%wide.region_18.20_spmd.sunk | while | flops 135529568 | bytes 17834880 | solution.py:81
  773.1 2.2 fusion.413
  777.3 2.2 fusion.414
  785.5 2.3 fusion.416
  793.6 2.3 fusion.418
  797.6 2.3 fusion.419
  801.9 2.2 fusion.420
  804.1 132.6 %all-reduce.8.cloned.1.call-done = f32[2,1024,128]{2,1,0:T(8,128)} async-done(((f32[2,1024,128]{2,1,0:T(8,128)}), f32[2,1024,128]{2,1,0:T(8,128)}) %all-reduce.8.cloned.1.call-update) | async-done | bytes 1048592 | tf_op jit(solution)/shard_map/psum | solution.py:100
  938.2 16.2 %psum.70 = f32[128]{0:T(128)S(1)} all-reduce(f32[128]{0:T(128)S(1)} %multiply_reduce_fusion.1), channel_id=1, replica_groups=mesh['hyd'=4,'src'=8] {'src'}, use_global_device_ids=true, to_apply=%region_22.24 | all-reduce | flops 128 | bytes 1024 | tf_op jit(solution)/shard_map/psum | solution.py:101
  954.4 2.5 fusion.240
  958.0 37.4 %while.65 = (s32[]{:T(128)}, f32[2,8,128,128]{3,2,1,0:T(8,128)}, s32[]{:T(128)}, s32[24]{0:T(128)S(1)}, bf16[24,2,128,128]{3,2,0,1:T(8,128)(2,1)S(1)}, /*index=5...) while((s32[]{:T(128)}, f32[2,8,128,128]{3,2,1,0:T(8,128)}, ...), condition=%wide.region_24.26_spmd, body=%wide.region_23.25_spmd.sunk | while | flops 135529568 | bytes 17834880 | solution.py:47
  964.7 2.2 fusion.428
  968.6 2.3 fusion.429
  976.7 2.2 fusion.431
  980.8 2.2 fusion.432
  989.1 2.3 fusion.434
  995.5 34.7 %collective-permute-start.6 = (f32[2,1024,128]{2,1,0:T(8,128)}, f32[2,1024,128]{2,1,0:T(8,128)S(1)}, u32[]{:S(2)}, u32[]{:S(2)}) collective-permute-start(f32[2,1024,128]{2,1,0:T(8,128)} %bitcast.578), channel_id=1, source_target_pairs={{0,1},{1,0},{2,3},{3,2},{4,5},{5,4},{6,7},{7,6},{8,9},{9,8},{10,11... | collective-permute-start | bytes 3145736 | tf_op jit(solution)/shard_map/ppermute | solution.py:115
  1030.2 2.5 collective-permute-done.6
  1034.0 38.6 %collective-permute-start.7 = (f32[2,1024,128]{2,1,0:T(8,128)S(1)}, f32[2,1024,128]{2,1,0:T(8,128)S(1)}, u32[]{:S(2)}, u32[]{:S(2)}) collective-permute-start(f32[2,1024,128]{2,1,0:T(8,128)S(1)} %bitcast_add_fusion), channel_id=1, source_target_pairs={{0,2},{1,3},{2,0},{3,1},{4,6},{5,7},{6,4},{7,5},{8,10},{9,11},{10,... | collective-permute-start | bytes 3145736 | tf_op jit(solution)/shard_map/ppermute | solution.py:115
  1072.6 23.5 %collective-permute-done.7 = f32[2,1024,128]{2,1,0:T(8,128)S(1)} collective-permute-done((f32[2,1024,128]{2,1,0:T(8,128)S(1)}, f32[2,1024,128]{2,1,0:T(8,128)S(1)}, u32[]{:S(2)}, u32[]{:S(2)}) %collective-permute-start.7) | collective-permute-done | bytes 1048608 | tf_op jit(solution)/shard_map/ppermute | solution.py:115
  1096.2 2.4 collective-permute-start.8
  1098.6 45.7 %collective-permute-done.8 = f32[2,1024,128]{2,1,0:T(8,128)S(1)} collective-permute-done((f32[2,1024,128]{2,1,0:T(8,128)S(1)}, f32[2,1024,128]{2,1,0:T(8,128)S(1)}, u32[]{:S(2)}, u32[]{:S(2)}) %collective-permute-start.8) | collective-permute-done | bytes 1048608 | tf_op jit(solution)/shard_map/ppermute | solution.py:115
  1145.4 8.9 psum.71
  1154.3 3.6 multiply_subtract_fusion
  (140 shorter events, 102.5 us)
Async XLA Ops:
  7.2 144.0 %all-reduce.4.cloned.1.call-start = ((), (), s32[]{:S(2)}) async-start(), calls=%async_computation | async-start | bytes 2097152 | tf_op jit(solution)/shard_map/psum | solution.py:100
  7.9 2.7 copy-start.5
  10.6 0.7 copy-start.8
  10.6 0.7 copy-start.9
  39.6 1.0 copy-start
  40.6 497.1 %all-reduce.6.cloned.1.call-start = ((), (), s32[]{:S(2)}) async-start(), calls=%async_computation.1 | async-start | bytes 2097152 | tf_op jit(solution)/shard_map/psum | solution.py:100
  191.8 39.1 %collective-permute-start = (f32[2,1024,128]{2,1,0:T(8,128)}, f32[2,1024,128]{2,1,0:T(8,128)S(1)}, u32[]{:S(2)}, u32[]{:S(2)}) collective-permute-start(f32[2,1024,128]{2,1,0:T(8,128)} %bitcast.579), channel_id=1, source_target_pairs={{0,1},{1,0},{2,3},{3,2},{4,5},{5,4},{6,7},{7,6},{8,9},{9,8},{10,11... | collective-permute-start | bytes 3145736 | tf_op jit(solution)/shard_map/ppermute | solution.py:115
  232.3 62.7 %collective-permute-start.1 = (f32[2,1024,128]{2,1,0:T(8,128)S(1)}, f32[2,1024,128]{2,1,0:T(8,128)S(1)}, u32[]{:S(2)}, u32[]{:S(2)}) collective-permute-start(f32[2,1024,128]{2,1,0:T(8,128)S(1)} %bitcast_add_fusion.2), channel_id=1, source_target_pairs={{0,2},{1,3},{2,0},{3,1},{4,6},{5,7},{6,4},{7,5},{8,10},{9,11},{10,... | collective-permute-start | bytes 3145736 | tf_op jit(solution)/shard_map/ppermute | solution.py:115
  296.0 48.5 %collective-permute-start.2 = (f32[2,1024,128]{2,1,0:T(8,128)}, f32[2,1024,128]{2,1,0:T(8,128)}, u32[]{:S(2)}, u32[]{:S(2)}) collective-permute-start(f32[2,1024,128]{2,1,0:T(8,128)} %add.524), channel_id=1, source_target_pairs={{0,4},{1,5},{2,6},{3,7},{4,0},{5,1},{6,2},{7,3},{8,12},{9,13},{10,... | collective-permute-start | bytes 3145736 | tf_op jit(solution)/shard_map/ppermute | solution.py:115
  332.3 23.8 %copy-start.6 = (f32[2,1024,128]{2,1,0:T(8,128)S(1)}, f32[2,1024,128]{2,1,0:T(8,128)}, u32[]{:S(2)}) copy-start(f32[2,1024,128]{2,1,0:T(8,128)} %param.19) | copy-start | bytes 3145732
  400.9 154.6 %copy-start.1 = (f32[2,1024,128]{2,1,0:T(8,128)S(1)}, f32[2,1024,128]{2,1,0:T(8,128)}, u32[]{:S(2)}) copy-start(f32[2,1024,128]{2,1,0:T(8,128)} %all-reduce.4.cloned.1.call-done) | copy-start | bytes 3145732
  400.9 535.8 %all-reduce.8.cloned.1.call-start = ((), (), s32[]{:S(2)}) async-start(), calls=%async_computation.2 | async-start | bytes 2097152 | tf_op jit(solution)/shard_map/psum | solution.py:100
  596.4 37.5 %collective-permute-start.3 = (f32[2,1024,128]{2,1,0:T(8,128)}, f32[2,1024,128]{2,1,0:T(8,128)S(1)}, u32[]{:S(2)}, u32[]{:S(2)}) collective-permute-start(f32[2,1024,128]{2,1,0:T(8,128)} %bitcast.580), channel_id=1, source_target_pairs={{0,1},{1,0},{2,3},{3,2},{4,5},{5,4},{6,7},{7,6},{8,9},{9,8},{10,11... | collective-permute-start | bytes 3145736 | tf_op jit(solution)/shard_map/ppermute | solution.py:115
  635.2 62.3 %collective-permute-start.4 = (f32[2,1024,128]{2,1,0:T(8,128)S(1)}, f32[2,1024,128]{2,1,0:T(8,128)S(1)}, u32[]{:S(2)}, u32[]{:S(2)}) collective-permute-start(f32[2,1024,128]{2,1,0:T(8,128)S(1)} %bitcast_add_fusion.1), channel_id=1, source_target_pairs={{0,2},{1,3},{2,0},{3,1},{4,6},{5,7},{6,4},{7,5},{8,10},{9,11},{10,... | collective-permute-start | bytes 3145736 | tf_op jit(solution)/shard_map/ppermute | solution.py:115
  698.6 48.3 %collective-permute-start.5 = (f32[2,1024,128]{2,1,0:T(8,128)}, f32[2,1024,128]{2,1,0:T(8,128)}, u32[]{:S(2)}, u32[]{:S(2)}) collective-permute-start(f32[2,1024,128]{2,1,0:T(8,128)} %add.530), channel_id=1, source_target_pairs={{0,4},{1,5},{2,6},{3,7},{4,0},{5,1},{6,2},{7,3},{8,12},{9,13},{10,... | collective-permute-start | bytes 3145736 | tf_op jit(solution)/shard_map/ppermute | solution.py:115
  700.9 57.6 %copy-start.7 = (f32[2,1024,128]{2,1,0:T(8,128)S(1)}, f32[2,1024,128]{2,1,0:T(8,128)}, u32[]{:S(2)}) copy-start(f32[2,1024,128]{2,1,0:T(8,128)} %param.19) | copy-start | bytes 3145732
  804.1 150.3 %copy-start.2 = (f32[2,1024,128]{2,1,0:T(8,128)S(1)}, f32[2,1024,128]{2,1,0:T(8,128)}, u32[]{:S(2)}) copy-start(f32[2,1024,128]{2,1,0:T(8,128)} %all-reduce.4.cloned.1.call-done) | copy-start | bytes 3145732
  995.5 37.2 %collective-permute-start.6 = (f32[2,1024,128]{2,1,0:T(8,128)}, f32[2,1024,128]{2,1,0:T(8,128)S(1)}, u32[]{:S(2)}, u32[]{:S(2)}) collective-permute-start(f32[2,1024,128]{2,1,0:T(8,128)} %bitcast.578), channel_id=1, source_target_pairs={{0,1},{1,0},{2,3},{3,2},{4,5},{5,4},{6,7},{7,6},{8,9},{9,8},{10,11... | collective-permute-start | bytes 3145736 | tf_op jit(solution)/shard_map/ppermute | solution.py:115
  1034.0 62.0 %collective-permute-start.7 = (f32[2,1024,128]{2,1,0:T(8,128)S(1)}, f32[2,1024,128]{2,1,0:T(8,128)S(1)}, u32[]{:S(2)}, u32[]{:S(2)}) collective-permute-start(f32[2,1024,128]{2,1,0:T(8,128)S(1)} %bitcast_add_fusion), channel_id=1, source_target_pairs={{0,2},{1,3},{2,0},{3,1},{4,6},{5,7},{6,4},{7,5},{8,10},{9,11},{10,... | collective-permute-start | bytes 3145736 | tf_op jit(solution)/shard_map/ppermute | solution.py:115
  1096.2 58.2 %copy-start.3 = (f32[2,1024,128]{2,1,0:T(8,128)S(1)}, f32[2,1024,128]{2,1,0:T(8,128)}, u32[]{:S(2)}) copy-start(f32[2,1024,128]{2,1,0:T(8,128)} %all-reduce.4.cloned.1.call-done) | copy-start | bytes 3145732
  1096.2 58.2 %copy-start.4 = (f32[2,1024,128]{2,1,0:T(8,128)S(1)}, f32[2,1024,128]{2,1,0:T(8,128)}, u32[]{:S(2)}) copy-start(f32[2,1024,128]{2,1,0:T(8,128)} %all-reduce.6.cloned.1.call-done) | copy-start | bytes 3145732
  1096.2 48.1 %collective-permute-start.8 = (f32[2,1024,128]{2,1,0:T(8,128)S(1)}, f32[2,1024,128]{2,1,0:T(8,128)S(1)}, u32[]{:S(2)}, u32[]{:S(2)}) collective-permute-start(f32[2,1024,128]{2,1,0:T(8,128)S(1)} %add.537), channel_id=1, source_target_pairs={{0,4},{1,5},{2,6},{3,7},{4,0},{5,1},{6,2},{7,3},{8,12},{9,13},{10,... | collective-permute-start | bytes 3145736 | tf_op jit(solution)/shard_map/ppermute | solution.py:115
Sparse Core Ops, SparseCore 0:
  40.7 110.4 all-reduce.3
  401.0 136.6 all-reduce.5
  804.2 132.4 all-reduce.7
